TPU v7x, 32 devices: a whole 2x2x4 slice. The times are simulated.
32 devices in a mesh: parts: 2 (over y), seq: 8 (over z, core), rep: 2 (over x), head: 1.
Axes of the slice: x: 2, y: 2, z: 4, core: 2. Of those that a mesh axis runs over, the one named last changes fastest.
Arguments:
- activations: bfloat16 [4, 1024, 2048], P(('parts', 'rep'), 'seq', 'head'), parts along dimension 0, may hold values from -6 to 6
- value_weight: bfloat16 [2048, 2048], P(('seq', 'rep'), 'head'), may hold values from -0.125 to 0.125
- query_in: bfloat16 [4, 1024, 2048], P(('parts', 'rep'), 'seq', 'head'), parts along dimension 0, may hold values from -6 to 6
- key_in: bfloat16 [4, 1024, 2048], P(('parts', 'rep'), 'seq', 'head'), parts along dimension 0, may hold values from -6 to 6
- grad_out: bfloat16 [4, 1024, 2048], P(('parts', 'rep'), 'seq', 'head'), parts along dimension 0, may hold values from -6 to 6
- conv_kernel: float32 [3, 4, 2048], P(None, None, 'head'), may hold values from -3 to 3
- log_gate: float32 [4, 16, 1024], P(('parts', 'rep'), 'head', 'seq'), parts along dimension 0, as said below
Outputs:
- attn_out: bfloat16 [4, 1024, 2048], P(('parts', 'rep'), 'seq', 'head'), parts along dimension 0
- grad_query: bfloat16 [4, 1024, 2048], P(('parts', 'rep'), 'seq', 'head'), parts along dimension 0
- grad_key: bfloat16 [4, 1024, 2048], P(('parts', 'rep'), 'seq', 'head'), parts along dimension 0
- grad_x: bfloat16 [4, 1024, 2048], P(('parts', 'rep'), 'seq', 'head'), parts along dimension 0
- grad_w: float32 [4096, 2048], P(('parts', 'seq', 'rep'), 'head'), parts along dimension 0
- grad_conv: float32 [6, 4, 2048], P('parts', None, 'head'), parts along dimension 0
There are 2 independent parts, one for each index of `parts`. A program takes and returns all parts, laid end to end along the dimension named above; an argument that names none is the same for every part. Nothing has to cross between parts.
Inputs may be any that keep to these rules, and one draw needn't show every extreme that they name: `log_gate`: every entry is below zero.
All inputs are finite; a program needn't handle non-finite values.
Results may differ from a plain program's by a relative error of at most 0.015.
Values may be sent and summed in bfloat16 or wider, within the bound.
A program may use at most 128 MiB of HBM per device.

v0:
```python
import math
import jax
import jax.numpy as jnp
from jax import lax
from jax.sharding import PartitionSpec as P

EPSILON = 1e-06


def shifted(block, axis, distance):
    devices = range(lax.axis_size(axis))
    route = [(i - distance, i) for i in devices if i - distance in devices]
    return lax.ppermute(block, axis, route)


def prefix(part, axis, combine, identity, reverse):
    count = lax.axis_size(axis)
    place = lax.axis_index(axis)
    ahead = count - 1 - place if reverse else place
    gathered = jax.tree.map(lambda a: lax.all_gather(a, axis), part)
    state = jax.tree.map(lambda a, e: jnp.zeros_like(a) + jnp.asarray(e, a.dtype), part, identity)

    def one(step, state):
        source = count - 1 - step if reverse else step
        return combine(
            state, jax.tree.map(lambda a: lax.dynamic_index_in_dim(a, source, 0, False), gathered)
        )

    return lax.fori_loop(0, ahead, one, state)


def carried_in(value, axis, combine, identity, reverse):
    length, mine = (lax.axis_size(axis), lax.axis_index(axis))
    everything = jax.tree.map(
        lambda part, kind: lax.all_gather(part.astype(kind), axis),
        value,
        (jnp.bfloat16, jnp.bfloat16),
    )
    start = jax.tree.map(
        lambda part, zero: jnp.broadcast_to(jnp.asarray(zero, part.dtype), part.shape),
        value,
        identity,
    )

    def step(k, before):
        at = length - 1 - k if reverse else k
        reached = at > mine if reverse else at < mine
        new = combine(
            before, jax.tree.map(lambda part, own: part[at].astype(own.dtype), everything, value)
        )
        return jax.tree.map(lambda a, b: jnp.where(reached, a, b), new, before)

    return lax.fori_loop(0, length, step, start)


def scanned(decay, state, axis, reverse):
    count = lax.axis_size(axis)
    direction = -1 if reverse else 1
    distance = 1
    while distance < count:
        far_decay, far_state = shifted((decay, state), axis, direction * distance)
        decay, state = chain_join((far_decay, far_state), (decay, state))
        distance *= 2
    return shifted(state, axis, direction)


def chain_join(earlier, following):
    return (earlier[0] * following[0], following[0][:, None, None] * earlier[1] + following[1])


def causal_filter(stream_rows, previous, kernel_taps):
    rim_rows = previous.shape[0]
    length = stream_rows.shape[0]
    extended = jnp.concatenate([previous, stream_rows], axis=0).astype(jnp.float32)
    result = jnp.zeros(stream_rows.shape, jnp.float32)
    for offset in range(kernel_taps.shape[0]):
        result = (
            result + kernel_taps[offset] * extended[rim_rows - offset : rim_rows - offset + length]
        )
    return result


def filter_back(post_rows, following_rows, kernel_taps):
    length = post_rows.shape[0]
    extended = jnp.concatenate([post_rows, following_rows], axis=0)
    result = jnp.zeros(post_rows.shape, jnp.float32)
    for offset in range(kernel_taps.shape[0]):
        result = result + kernel_taps[offset] * extended[offset : offset + length]
    return result


def tap_sums(post_rows, stream_rows, previous, kernel_width):
    rim_rows = previous.shape[0]
    length = stream_rows.shape[0]
    extended = jnp.concatenate([previous, stream_rows], axis=0).astype(jnp.float32)
    return jnp.stack(
        [
            jnp.sum(post_rows * extended[rim_rows - offset : rim_rows - offset + length], axis=0)
            for offset in range(kernel_width)
        ]
    )


def local(activations, value_weight, query_in, key_in, grad_out, conv_kernel, log_gate):
    tok_rows = query_in.shape[1]
    channels = query_in.shape[2]
    head_count = log_gate.shape[1]
    head_size = channels // head_count
    kernel_width = conv_kernel.shape[1]
    rim_rows = kernel_width - 1
    grad_scale = 1.0 / math.sqrt(lax.axis_size("seq") * lax.axis_size("rep") * tok_rows)
    query_rows = query_in[0]
    key_rows = key_in[0]
    gathered = lax.all_gather(activations, "head", axis=2, tiled=True)[0]
    columns = gathered
    value_f32 = jnp.dot(
        columns,
        lax.all_gather(value_weight, ("seq", "rep"), axis=0, tiled=True),
        preferred_element_type=jnp.float32,
    )
    value_raw = value_f32.astype(jnp.bfloat16)
    before_all = shifted(
        jnp.stack(
            [
                query_rows[tok_rows - rim_rows :],
                key_rows[tok_rows - rim_rows :],
                value_raw[tok_rows - rim_rows :],
            ]
        ),
        "seq",
        1,
    )
    before = (before_all[0], before_all[1], before_all[2])
    raw_rows = (query_rows, key_rows, value_raw)
    convolved = [
        causal_filter(raw_rows[which], before[which], conv_kernel[which]).astype(jnp.bfloat16)
        for which in range(3)
    ]
    query_heads = convolved[0].reshape(tok_rows, head_count, head_size)
    key_heads = convolved[1].reshape(tok_rows, head_count, head_size)
    value_heads = convolved[2].reshape(tok_rows, head_count, head_size)
    cumulative = jnp.cumsum(log_gate[0], axis=1)
    final_cum = cumulative[:, -1]
    block_decay = jnp.exp(final_cum)
    rising = jnp.exp(cumulative).T[:, :, None]
    shrink = jnp.exp(final_cum[:, None] - cumulative).T[:, :, None]
    mixing = jnp.exp(-jnp.abs(cumulative[:, :, None] - cumulative[:, None, :]))
    scores = (
        mixing
        * jnp.einsum("thd,shd->hts", query_heads, key_heads, preferred_element_type=jnp.float32)
    ).astype(jnp.bfloat16)
    fwd_sum = jnp.einsum(
        "thd,the->hde",
        (shrink * key_heads).astype(jnp.bfloat16),
        value_heads,
        preferred_element_type=jnp.float32,
    )
    back_sum = jnp.einsum(
        "thd,the->hde",
        (rising * key_heads).astype(jnp.bfloat16),
        value_heads,
        preferred_element_type=jnp.float32,
    )
    identity = (
        jnp.ones((head_count,), jnp.float32),
        jnp.zeros((head_count, head_size, head_size), jnp.float32),
    )
    left_b = scanned(block_decay, fwd_sum, "seq", False).astype(jnp.bfloat16)
    right_b = scanned(block_decay, back_sum, "seq", True).astype(jnp.bfloat16)
    attn = rising * jnp.einsum(
        "thd,hde->the", query_heads, left_b, preferred_element_type=jnp.float32
    )
    attn = attn + shrink * jnp.einsum(
        "thd,hde->the", query_heads, right_b, preferred_element_type=jnp.float32
    )
    attn = attn + jnp.einsum(
        "hts,she->the", scores, value_heads, preferred_element_type=jnp.float32
    )
    root_mean = jnp.sqrt(jnp.mean(attn * attn, axis=2, keepdims=True) + EPSILON)
    normed = attn / root_mean
    attn_out = normed.astype(jnp.bfloat16).reshape(1, tok_rows, channels)
    upstream = grad_out[0].reshape(tok_rows, head_count, head_size).astype(jnp.float32)
    grad_attn = (
        (upstream - normed * jnp.mean(upstream * normed, axis=2, keepdims=True)) / root_mean
    ).astype(jnp.bfloat16)
    grad_scores = (
        mixing
        * jnp.einsum("the,she->hts", grad_attn, value_heads, preferred_element_type=jnp.float32)
    ).astype(jnp.bfloat16)
    fwd_grad = jnp.einsum(
        "thd,the->hde",
        (shrink * query_heads).astype(jnp.bfloat16),
        grad_attn,
        preferred_element_type=jnp.float32,
    )
    back_grad = jnp.einsum(
        "thd,the->hde",
        (rising * query_heads).astype(jnp.bfloat16),
        grad_attn,
        preferred_element_type=jnp.float32,
    )
    left_gb = scanned(block_decay, fwd_grad, "seq", False).astype(jnp.bfloat16)
    right_gb = scanned(block_decay, back_grad, "seq", True).astype(jnp.bfloat16)
    query_post = rising * jnp.einsum(
        "the,hde->thd", grad_attn, left_b, preferred_element_type=jnp.float32
    )
    query_post = query_post + shrink * jnp.einsum(
        "the,hde->thd", grad_attn, right_b, preferred_element_type=jnp.float32
    )
    query_post = query_post + jnp.einsum(
        "hts,shd->thd", grad_scores, key_heads, preferred_element_type=jnp.float32
    )
    key_post = rising * jnp.einsum(
        "the,hde->thd", value_heads, left_gb, preferred_element_type=jnp.float32
    )
    key_post = key_post + shrink * jnp.einsum(
        "the,hde->thd", value_heads, right_gb, preferred_element_type=jnp.float32
    )
    key_post = key_post + jnp.einsum(
        "hts,thd->shd", grad_scores, query_heads, preferred_element_type=jnp.float32
    )
    value_post = rising * jnp.einsum(
        "thd,hde->the", key_heads, left_gb, preferred_element_type=jnp.float32
    )
    value_post = value_post + shrink * jnp.einsum(
        "thd,hde->the", key_heads, right_gb, preferred_element_type=jnp.float32
    )
    value_post = value_post + jnp.einsum(
        "hts,the->she", scores, grad_attn, preferred_element_type=jnp.float32
    )
    post_grads = jnp.stack(
        [
            query_post.reshape(tok_rows, channels),
            key_post.reshape(tok_rows, channels),
            value_post.reshape(tok_rows, channels),
        ]
    )
    following = shifted(post_grads[:, :rim_rows].astype(jnp.bfloat16), "seq", -1).astype(
        jnp.float32
    )
    grad_query = filter_back(post_grads[0], following[0], conv_kernel[0]).astype(jnp.bfloat16)
    grad_key = filter_back(post_grads[1], following[1], conv_kernel[1]).astype(jnp.bfloat16)
    grad_value = filter_back(post_grads[2], following[2], conv_kernel[2]).astype(jnp.bfloat16)
    kernel_terms = (
        jnp.stack(
            [
                tap_sums(post_grads[which], raw_rows[which], before[which], kernel_width)
                for which in range(3)
            ]
        )
        * grad_scale
    )
    grad_conv = lax.psum(kernel_terms, ("seq", "rep"))
    partial_x = lax.dot_general(
        grad_value,
        lax.all_gather(value_weight, ("seq", "rep"), axis=0, tiled=True),
        (((1,), (1,)), ((), ())),
        preferred_element_type=jnp.float32,
    )
    grad_x = lax.psum_scatter(
        partial_x[None].astype(jnp.bfloat16), "head", scatter_dimension=2, tiled=True
    )
    feature_rows = lax.all_to_all(gathered, ("seq", "rep"), 1, 0, tiled=True)
    grad_value_all = lax.all_gather(grad_value, ("seq", "rep"), axis=0, tiled=True)
    grad_w = (
        lax.dot_general(
            feature_rows,
            grad_value_all,
            (((0,), (0,)), ((), ())),
            preferred_element_type=jnp.float32,
        )
        * grad_scale
    )
    return (attn_out, grad_query[None], grad_key[None], grad_x, grad_w, grad_conv)


def solution(mesh):
    placed = (
        P(("parts", "rep"), "seq", "head"),
        P(("seq", "rep"), "head"),
        P(("parts", "rep"), "seq", "head"),
        P(("parts", "rep"), "seq", "head"),
        P(("parts", "rep"), "seq", "head"),
        P(None, None, "head"),
        P(("parts", "rep"), "head", "seq"),
    )
    return jax.shard_map(
        local,
        mesh=mesh,
        in_specs=placed,
        out_specs=(
            P(("parts", "rep"), "seq", "head"),
            P(("parts", "rep"), "seq", "head"),
            P(("parts", "rep"), "seq", "head"),
            P(("parts", "rep"), "seq", "head"),
            P(("parts", "seq", "rep"), "head"),
            P("parts", None, "head"),
        ),
        check_vma=False,
    )
```

profile of v0, /device:TPU:0, one launch (start us, length us, event | category | flops | bytes accessed | tf_op | source)
XLA Modules:
  0.0 546.2 jit_solution(14763116871213756074)
XLA Ops:
  11.9 75.3 %all-gather.3.cloned.1.call-done = bf16[2048,2048]{1,0:T(8,128)(2,1)} async-done(((bf16[128,2048]{1,0:T(8,128)(2,1)}), bf16[2048,2048]{1,0:T(8,128)(2,1)}) %all-gather.3.cloned.1.call-update) | async-done | bytes 8388624 | tf_op jit(solution)/shard_map/all_gather | solution.py:118
  87.2 4.6 convolution_convert_fusion.1
  92.0 2.2 collective-permute-start.2
  99.4 3.4 collective-permute-start.3
  105.0 4.4 collective-permute-done.9
  111.2 14.4 %collective-permute-start.4 = (f32[16,128,128]{2,1,0:T(8,128)S(1)}, f32[16,128,128]{2,1,0:T(8,128)S(1)}, u32[]{:S(2)}, u32[]{:S(2)}) collective-permute-start(f32[16,128,128]{2,1,0:T(8,128)S(1)} %get-tuple-element.65), channel_id=1, source_target_pairs={{0,4},{2,6},{4,8},{6,10},{8,12},{10,14},{1,5},{3,7},{5,9},{7,11},{... | collective-permute-start | bytes 3145736 | tf_op jit(solution)/shard_map/ppermute | solution.py:13
  125.6 3.6 collective-permute-start
  130.6 1.7 collective-permute-done.7
  132.3 14.0 %collective-permute-done.10 = f32[16,128,128]{2,1,0:T(8,128)S(1)} collective-permute-done((f32[16,128,128]{2,1,0:T(8,128)S(1)}, f32[16,128,128]{2,1,0:T(8,128)S(1)}, u32[]{:S(2)}, u32[]{:S(2)}) %collective-permute-start.10) | collective-permute-done | bytes 1048608 | tf_op jit(solution)/shard_map/ppermute | solution.py:13
  150.0 10.6 %collective-permute-start.5 = (f32[16,128,128]{2,1,0:T(8,128)}, f32[16,128,128]{2,1,0:T(8,128)}, u32[]{:S(2)}, u32[]{:S(2)}) collective-permute-start(f32[16,128,128]{2,1,0:T(8,128)} %multiply_add_fusion.10), channel_id=1, source_target_pairs={{0,8},{2,10},{4,12},{6,14},{1,9},{3,11},{5,13},{7,15},{16,24},{18,... | collective-permute-start | bytes 3145736 | tf_op jit(solution)/shard_map/ppermute | solution.py:13
  160.6 2.2 copy.108
  162.8 4.0 collective-permute-start.1
  168.1 13.9 %collective-permute-done.1 = f32[16]{0:T(128)S(1)} collective-permute-done((f32[16]{0:T(128)S(1)}, f32[16]{0:T(128)S(1)}, u32[]{:S(2)}, u32[]{:S(2)}) %collective-permute-start.1) | collective-permute-done | bytes 96 | tf_op jit(solution)/shard_map/ppermute | solution.py:13
  183.3 2.0 copy.99
  185.3 1.7 fusion.18
  187.1 14.1 %collective-permute-done.11 = f32[16,128,128]{2,1,0:T(8,128)} collective-permute-done((f32[16,128,128]{2,1,0:T(8,128)}, f32[16,128,128]{2,1,0:T(8,128)}, u32[]{:S(2)}, u32[]{:S(2)}) %collective-permute-start.11) | collective-permute-done | bytes 1048608 | tf_op jit(solution)/shard_map/ppermute | solution.py:13
  201.2 1.7 multiply_add_fusion.6
  204.3 1.7 multiply_add_fusion.9
  206.1 3.2 collective-permute-start.6
  213.6 16.0 %collective-permute-start.13 = (f32[16,128,128]{2,1,0:T(8,128)S(1)}, f32[16,128,128]{2,1,0:T(8,128)S(1)}, u32[]{:S(2)}, u32[]{:S(2)}) collective-permute-start(f32[16,128,128]{2,1,0:T(8,128)S(1)} %fusion.53), channel_id=1, source_target_pairs={{0,2},{2,4},{4,6},{6,8},{8,10},{10,12},{12,14},{1,3},{3,5},{5,7},{... | collective-permute-start | bytes 3145736 | tf_op jit(solution)/shard_map/ppermute | solution.py:13
  231.8 4.3 collective-permute-done.17
  238.0 14.6 %collective-permute-start.14 = (f32[16,128,128]{2,1,0:T(8,128)S(1)}, f32[16,128,128]{2,1,0:T(8,128)S(1)}, u32[]{:S(2)}, u32[]{:S(2)}) collective-permute-start(f32[16,128,128]{2,1,0:T(8,128)S(1)} %get-tuple-element.61), channel_id=1, source_target_pairs={{0,4},{2,6},{4,8},{6,10},{8,12},{10,14},{1,5},{3,7},{5,9},{7,11},{... | collective-permute-start | bytes 3145736 | tf_op jit(solution)/shard_map/ppermute | solution.py:13
  253.4 19.0 %collective-permute-done.18 = f32[16,128,128]{2,1,0:T(8,128)S(1)} collective-permute-done((f32[16,128,128]{2,1,0:T(8,128)S(1)}, f32[16,128,128]{2,1,0:T(8,128)S(1)}, u32[]{:S(2)}, u32[]{:S(2)}) %collective-permute-start.18) | collective-permute-done | bytes 1048608 | tf_op jit(solution)/shard_map/ppermute | solution.py:13
  276.2 9.0 %collective-permute-start.15 = (f32[16,128,128]{2,1,0:T(8,128)}, f32[16,128,128]{2,1,0:T(8,128)}, u32[]{:S(2)}, u32[]{:S(2)}) collective-permute-start(f32[16,128,128]{2,1,0:T(8,128)} %multiply_add_fusion.4), channel_id=1, source_target_pairs={{0,8},{2,10},{4,12},{6,14},{1,9},{3,11},{5,13},{7,15},{16,24},{18,... | collective-permute-start | bytes 3145736 | tf_op jit(solution)/shard_map/ppermute | solution.py:13
  287.2 2.0 copy.156
  290.8 36.1 %collective-permute-done.19 = f32[16,128,128]{2,1,0:T(8,128)} collective-permute-done((f32[16,128,128]{2,1,0:T(8,128)}, f32[16,128,128]{2,1,0:T(8,128)}, u32[]{:S(2)}, u32[]{:S(2)}) %collective-permute-start.19) | collective-permute-done | bytes 1048608 | tf_op jit(solution)/shard_map/ppermute | solution.py:13
  326.9 1.7 multiply_add_fusion
  330.1 1.7 multiply_add_fusion.3
  331.8 3.2 collective-permute-start.16
  336.9 1.7 fusion.90
  338.6 2.0 copy.157
  340.6 1.7 fusion.2
  342.5 1.5 fusion.89
  344.0 2.0 copy.158
  348.1 2.6 copy.159
  350.7 4.3 collective-permute-done.21
  355.0 4.4 multiply_reduce_fusion.3
  359.5 2.0 copy.129
  361.5 29.8 %all_to_all.19 = bf16[128,16,128]{0,2,1:T(8,128)(2,1)} all-to-all(bf16[128,16,128]{0,2,1:T(8,128)(2,1)} %bitcast.200), channel_id=1, replica_groups=mesh['parts'=2,'seq'=8,'rep'=2,'head'=1] {'seq','rep'}, dimensions={1} | all-to-all | bytes 1048576 | tf_op jit(solution)/shard_map/all_to_all | solution.py:263
  391.3 2.0 copy.130
  394.7 2.1 copy.139
  398.2 4.1 multiply_reduce_fusion.11
  402.4 1.7 multiply_reduce_fusion.7
  404.9 8.2 %fusion.1 = bf16[1,128,2048]{2,1,0:T(8,128)(2,1)} fusion(bf16[128,2048]{1,0:T(8,128)(2,1)S(1)} %copy-done.10, bf16[2048,2048]{1,0:T(8,128)(2,1)} %all-gather.3.cloned.1.call-done), kind=kOutput, calls=%fused_computation.4 | convolution fusion | flops 1074003968 | bytes 9437184 | tf_op jit(solution)/shard_map/dot_general | solution.py:254
  413.1 33.6 %all-gather.5.cloned.1.call-done = bf16[2048,2048]{1,0:T(8,128)(2,1)} async-done(((bf16[128,2048]{1,0:T(8,128)(2,1)}), bf16[2048,2048]{1,0:T(8,128)(2,1)}) %all-gather.5.cloned.1.call-update) | async-done | bytes 8388624 | tf_op jit(solution)/shard_map/all_gather | solution.py:264
  446.7 5.8 %fusion = f32[128,2048]{0,1:T(8,128)S(1)} fusion(bf16[2048,2048]{1,0:T(8,128)(2,1)} %all-gather.5.cloned.1.call-done, bf16[2048,128]{1,0:T(8,128)(2,1)S(1)} %bitcast.204), kind=kOutput, calls=%fused_computation.1 | convolution fusion | flops 1074003968 | bytes 9961472 | tf_op jit(solution)/shard_map/dot_general | solution.py:266
  453.8 84.3 %all-reduce.2.cloned.1.call-done = f32[3,4,2048]{2,1,0:T(4,128)} async-done(((f32[3,4,2048]{2,1,0:T(4,128)}), f32[3,4,2048]{2,1,0:T(4,128)}) %all-reduce.2.cloned.1.call-update) | async-done | bytes 98320 | tf_op jit(solution)/shard_map/psum | solution.py:253
  538.1 1.5 copy.188
  (135 shorter events, 49.7 us)
Async XLA Ops:
  7.2 80.1 %copy-start.15 = (bf16[1,128,2048]{2,1,0:T(8,128)(2,1)S(1)}, bf16[1,128,2048]{2,1,0:T(8,128)(2,1)}, u32[]{:S(2)}) copy-start(bf16[1,128,2048]{2,1,0:T(8,128)(2,1)} %param.7) | copy-start | bytes 1572868
  7.2 80.1 %all-gather.3.cloned.1.call-start = ((), (), s32[]{:S(2)}) async-start(), calls=%async_computation.1 | async-start | bytes 8912896 | tf_op jit(solution)/shard_map/all_gather | solution.py:118
  7.9 438.8 %all-gather.5.cloned.1.call-start = ((), (), s32[]{:S(2)}) async-start(), calls=%async_computation.2 | async-start | bytes 8912896 | tf_op jit(solution)/shard_map/all_gather | solution.py:264
  11.9 83.2 %copy-start.23 = (bf16[1,128,2048]{2,1,0:T(8,128)(2,1)S(1)}, bf16[1,128,2048]{2,1,0:T(8,128)(2,1)}, u32[]{:S(2)}) copy-start(bf16[1,128,2048]{2,1,0:T(8,128)(2,1)} %param.10) | copy-start | bytes 1572868
  11.9 83.2 %copy-start.24 = (bf16[1,128,2048]{2,1,0:T(8,128)(2,1)S(1)}, bf16[1,128,2048]{2,1,0:T(8,128)(2,1)}, u32[]{:S(2)}) copy-start(bf16[1,128,2048]{2,1,0:T(8,128)(2,1)} %param.9) | copy-start | bytes 1572868
  91.9 3.1 copy-start.16
  92.0 3.0 collective-permute-start.2
  98.5 4.5 copy-start
  99.4 5.6 %collective-permute-start.3 = (f32[16,128,128]{2,1,0:T(8,128)S(1)}, f32[16,128,128]{2,1,0:T(8,128)S(1)}, u32[]{:S(2)}, u32[]{:S(2)}) collective-permute-start(f32[16,128,128]{2,1,0:T(8,128)S(1)} %fusion.57), channel_id=1, source_target_pairs={{0,2},{2,4},{4,6},{6,8},{8,10},{10,12},{12,14},{1,3},{3,5},{5,7},{... | collective-permute-start | bytes 3145736 | tf_op jit(solution)/shard_map/ppermute | solution.py:13
  103.1 6.3 %collective-permute-start.9 = (f32[16,128,128]{2,1,0:T(8,128)S(1)}, f32[16,128,128]{2,1,0:T(8,128)S(1)}, u32[]{:S(2)}, u32[]{:S(2)}) collective-permute-start(f32[16,128,128]{2,1,0:T(8,128)S(1)} %fusion.55), channel_id=1, source_target_pairs={{2,0},{4,2},{6,4},{8,6},{10,8},{12,10},{14,12},{3,1},{5,3},{7,5},{... | collective-permute-start | bytes 3145736 | tf_op jit(solution)/shard_map/ppermute | solution.py:13
  109.9 36.4 %collective-permute-start.10 = (f32[16,128,128]{2,1,0:T(8,128)S(1)}, f32[16,128,128]{2,1,0:T(8,128)S(1)}, u32[]{:S(2)}, u32[]{:S(2)}) collective-permute-start(f32[16,128,128]{2,1,0:T(8,128)S(1)} %get-tuple-element.66), channel_id=1, source_target_pairs={{4,0},{6,2},{8,4},{10,6},{12,8},{14,10},{5,1},{7,3},{9,5},{11,7},{... | collective-permute-start | bytes 3145736 | tf_op jit(solution)/shard_map/ppermute | solution.py:13
  111.2 37.6 %collective-permute-start.4 = (f32[16,128,128]{2,1,0:T(8,128)S(1)}, f32[16,128,128]{2,1,0:T(8,128)S(1)}, u32[]{:S(2)}, u32[]{:S(2)}) collective-permute-start(f32[16,128,128]{2,1,0:T(8,128)S(1)} %get-tuple-element.65), channel_id=1, source_target_pairs={{0,4},{2,6},{4,8},{6,10},{8,12},{10,14},{1,5},{3,7},{5,9},{7,11},{... | collective-permute-start | bytes 3145736 | tf_op jit(solution)/shard_map/ppermute | solution.py:13
  125.6 4.9 collective-permute-start
  129.3 3.1 collective-permute-start.7
  147.6 53.6 %collective-permute-start.11 = (f32[16,128,128]{2,1,0:T(8,128)}, f32[16,128,128]{2,1,0:T(8,128)}, u32[]{:S(2)}, u32[]{:S(2)}) collective-permute-start(f32[16,128,128]{2,1,0:T(8,128)} %multiply_add_fusion.7), channel_id=1, source_target_pairs={{8,0},{10,2},{12,4},{14,6},{9,1},{11,3},{13,5},{15,7},{24,16},{26,... | collective-permute-start | bytes 3145736 | tf_op jit(solution)/shard_map/ppermute | solution.py:13
  150.0 54.3 %collective-permute-start.5 = (f32[16,128,128]{2,1,0:T(8,128)}, f32[16,128,128]{2,1,0:T(8,128)}, u32[]{:S(2)}, u32[]{:S(2)}) collective-permute-start(f32[16,128,128]{2,1,0:T(8,128)} %multiply_add_fusion.10), channel_id=1, source_target_pairs={{0,8},{2,10},{4,12},{6,14},{1,9},{3,11},{5,13},{7,15},{16,24},{18,... | collective-permute-start | bytes 3145736 | tf_op jit(solution)/shard_map/ppermute | solution.py:13
  162.8 19.2 %collective-permute-start.1 = (f32[16]{0:T(128)S(1)}, f32[16]{0:T(128)S(1)}, u32[]{:S(2)}, u32[]{:S(2)}) collective-permute-start(f32[16]{0:T(128)S(1)} %get-tuple-element.63), channel_id=1, source_target_pairs={{0,4},{2,6},{4,8},{6,10},{8,12},{10,14},{1,5},{3,7},{5,9},{7,11},{... | collective-permute-start | bytes 200 | tf_op jit(solution)/shard_map/ppermute | solution.py:13
  166.8 15.2 %collective-permute-start.8 = (f32[16]{0:T(128)S(1)}, f32[16]{0:T(128)S(1)}, u32[]{:S(2)}, u32[]{:S(2)}) collective-permute-start(f32[16]{0:T(128)S(1)} %get-tuple-element.64), channel_id=1, source_target_pairs={{4,0},{6,2},{8,4},{10,6},{12,8},{14,10},{5,1},{7,3},{9,5},{11,7},{... | collective-permute-start | bytes 200 | tf_op jit(solution)/shard_map/ppermute | solution.py:13
  187.1 22.2 %copy-start.19 = (bf16[16,128,128]{2,1,0:T(8,128)(2,1)}, bf16[16,128,128]{2,1,0:T(8,128)(2,1)S(1)}, u32[]{:S(2)}) copy-start(bf16[16,128,128]{2,1,0:T(8,128)(2,1)S(1)} %fusion.18) | copy-start | bytes 1572868
  202.9 6.4 %copy-start.1 = (bf16[16,16,8,128]{3,2,1,0:T(8,128)(2,1)S(1)}, bf16[16,16,8,128]{3,2,1,0:T(8,128)(2,1)}, u32[]{:S(2)}) copy-start(bf16[16,16,8,128]{3,2,1,0:T(8,128)(2,1)} %copy-done) | copy-start | bytes 1572868
  202.9 6.9 %collective-permute-start.12 = (bf16[16,128,128]{2,1,0:T(8,128)(2,1)S(1)}, bf16[16,128,128]{2,1,0:T(8,128)(2,1)S(1)}, u32[]{:S(2)}, u32[]{:S(2)}) collective-permute-start(bf16[16,128,128]{2,1,0:T(8,128)(2,1)S(1)} %multiply_add_fusion.6), channel_id=1, source_target_pairs={{2,0},{4,2},{6,4},{8,6},{10,8},{12,10},{14,12},{3,1},{5,3},{7,5},{... | collective-permute-start | bytes 1572872 | tf_op jit(solution)/shard_map/ppermute | solution.py:13
  206.1 3.8 copy-start.8
  206.1 4.7 collective-permute-start.6
  212.6 73.1 %copy-start.6 = (bf16[128,16,128]{0,2,1:T(8,128)(2,1)}, bf16[128,16,128]{0,2,1:T(8,128)(2,1)S(1)}, u32[]{:S(2)}) copy-start(bf16[128,16,128]{0,2,1:T(8,128)(2,1)S(1)} %get-tuple-element.36) | copy-start | bytes 1572868
  213.6 18.2 %collective-permute-start.13 = (f32[16,128,128]{2,1,0:T(8,128)S(1)}, f32[16,128,128]{2,1,0:T(8,128)S(1)}, u32[]{:S(2)}, u32[]{:S(2)}) collective-permute-start(f32[16,128,128]{2,1,0:T(8,128)S(1)} %fusion.53), channel_id=1, source_target_pairs={{0,2},{2,4},{4,6},{6,8},{8,10},{10,12},{12,14},{1,3},{3,5},{5,7},{... | collective-permute-start | bytes 3145736 | tf_op jit(solution)/shard_map/ppermute | solution.py:13
  229.6 6.5 %collective-permute-start.17 = (f32[16,128,128]{2,1,0:T(8,128)S(1)}, f32[16,128,128]{2,1,0:T(8,128)S(1)}, u32[]{:S(2)}, u32[]{:S(2)}) collective-permute-start(f32[16,128,128]{2,1,0:T(8,128)S(1)} %fusion.51), channel_id=1, source_target_pairs={{2,0},{4,2},{6,4},{8,6},{10,8},{12,10},{14,12},{3,1},{5,3},{7,5},{... | collective-permute-start | bytes 3145736 | tf_op jit(solution)/shard_map/ppermute | solution.py:13
  236.7 35.7 %collective-permute-start.18 = (f32[16,128,128]{2,1,0:T(8,128)S(1)}, f32[16,128,128]{2,1,0:T(8,128)S(1)}, u32[]{:S(2)}, u32[]{:S(2)}) collective-permute-start(f32[16,128,128]{2,1,0:T(8,128)S(1)} %get-tuple-element.62), channel_id=1, source_target_pairs={{4,0},{6,2},{8,4},{10,6},{12,8},{14,10},{5,1},{7,3},{9,5},{11,7},{... | collective-permute-start | bytes 3145736 | tf_op jit(solution)/shard_map/ppermute | solution.py:13
  238.0 37.1 %collective-permute-start.14 = (f32[16,128,128]{2,1,0:T(8,128)S(1)}, f32[16,128,128]{2,1,0:T(8,128)S(1)}, u32[]{:S(2)}, u32[]{:S(2)}) collective-permute-start(f32[16,128,128]{2,1,0:T(8,128)S(1)} %get-tuple-element.61), channel_id=1, source_target_pairs={{0,4},{2,6},{4,8},{6,10},{8,12},{10,14},{1,5},{3,7},{5,9},{7,11},{... | collective-permute-start | bytes 3145736 | tf_op jit(solution)/shard_map/ppermute | solution.py:13
  253.1 32.1 %copy-start.21 = (bf16[16,128,128]{2,1,0:T(8,128)(2,1)}, bf16[16,128,128]{2,1,0:T(8,128)(2,1)S(1)}, u32[]{:S(2)}) copy-start(bf16[16,128,128]{2,1,0:T(8,128)(2,1)S(1)} %fusion.19) | copy-start | bytes 1572868
  273.6 11.6 %copy-start.4 = (bf16[128,2048]{0,1:T(8,128)(2,1)S(1)}, bf16[128,2048]{0,1:T(8,128)(2,1)}, u32[]{:S(2)}) copy-start(bf16[128,2048]{0,1:T(8,128)(2,1)} %copy.97) | copy-start | bytes 1572868
  273.6 53.3 %collective-permute-start.19 = (f32[16,128,128]{2,1,0:T(8,128)}, f32[16,128,128]{2,1,0:T(8,128)}, u32[]{:S(2)}, u32[]{:S(2)}) collective-permute-start(f32[16,128,128]{2,1,0:T(8,128)} %multiply_add_fusion.1), channel_id=1, source_target_pairs={{8,0},{10,2},{12,4},{14,6},{9,1},{11,3},{13,5},{15,7},{24,16},{26,... | collective-permute-start | bytes 3145736 | tf_op jit(solution)/shard_map/ppermute | solution.py:13
  276.2 53.9 %collective-permute-start.15 = (f32[16,128,128]{2,1,0:T(8,128)}, f32[16,128,128]{2,1,0:T(8,128)}, u32[]{:S(2)}, u32[]{:S(2)}) collective-permute-start(f32[16,128,128]{2,1,0:T(8,128)} %multiply_add_fusion.4), channel_id=1, source_target_pairs={{0,8},{2,10},{4,12},{6,14},{1,9},{3,11},{5,13},{7,15},{16,24},{18,... | collective-permute-start | bytes 3145736 | tf_op jit(solution)/shard_map/ppermute | solution.py:13
  328.6 6.4 %copy-start.7 = (bf16[128,16,128]{0,2,1:T(8,128)(2,1)S(1)}, bf16[128,16,128]{0,2,1:T(8,128)(2,1)}, u32[]{:S(2)}) copy-start(bf16[128,16,128]{0,2,1:T(8,128)(2,1)} %copy-done.6) | copy-start | bytes 1572868
  328.6 6.4 %copy-start.20 = (bf16[16,128,128]{2,1,0:T(8,128)(2,1)S(1)}, bf16[16,128,128]{2,1,0:T(8,128)(2,1)}, u32[]{:S(2)}) copy-start(bf16[16,128,128]{2,1,0:T(8,128)(2,1)} %copy-done.19) | copy-start | bytes 1572868
  328.6 7.8 %collective-permute-start.20 = (bf16[16,128,128]{2,1,0:T(8,128)(2,1)S(1)}, bf16[16,128,128]{2,1,0:T(8,128)(2,1)S(1)}, u32[]{:S(2)}, u32[]{:S(2)}) collective-permute-start(bf16[16,128,128]{2,1,0:T(8,128)(2,1)S(1)} %multiply_add_fusion), channel_id=1, source_target_pairs={{2,0},{4,2},{6,4},{8,6},{10,8},{12,10},{14,12},{3,1},{5,3},{7,5},{... | collective-permute-start | bytes 1572872 | tf_op jit(solution)/shard_map/ppermute | solution.py:13
  331.8 4.6 copy-start.2
  331.8 5.1 collective-permute-start.16
  336.4 2.2 copy-start.22
  340.6 1.7 copy-start.5
  340.6 1.7 copy-start.14
  340.6 1.8 copy-start.18
  346.8 8.2 %collective-permute-start.21 = (bf16[3,3,2048]{2,1,0:T(4,128)(2,1)S(1)}, bf16[3,3,2048]{2,1,0:T(4,128)(2,1)S(1)}, u32[]{:S(2)}, u32[]{:S(2)}) collective-permute-start(bf16[3,3,2048]{2,1,0:T(4,128)(2,1)S(1)} %pad_maximum_fusion.3), channel_id=1, source_target_pairs={{2,0},{4,2},{6,4},{8,6},{10,8},{12,10},{14,12},{3,1},{5,3},{7,5},{... | collective-permute-start | bytes 110600 | tf_op jit(solution)/shard_map/ppermute | solution.py:13
  359.4 178.6 %all-reduce.2.cloned.1.call-start = ((), (), s32[]{:S(2)}) async-start(), calls=%async_computation.3 | async-start | bytes 196608 | tf_op jit(solution)/shard_map/psum | solution.py:253
  361.5 31.9 %copy-start.11 = (f32[128,16,128]{0,2,1:T(8,128)S(1)}, f32[128,16,128]{0,2,1:T(8,128)}, u32[]{:S(2)}) copy-start(f32[128,16,128]{0,2,1:T(8,128)} %get-tuple-element.74) | copy-start | bytes 3145732
  394.7 2.1 copy-start.12
  398.2 4.2 copy-start.13
  402.4 2.5 copy-start.10
  404.9 41.8 %copy-start.25 = (bf16[16,128,128]{2,1,0:T(8,128)(2,1)S(1)}, bf16[16,128,128]{2,1,0:T(8,128)(2,1)}, u32[]{:S(2)}) copy-start(bf16[16,128,128]{2,1,0:T(8,128)(2,1)} %copy.130) | copy-start | bytes 1572868
  (3 other events, 3.9 us)
Sparse Core Ops, SparseCore 0:
  10.2 76.9 all-gather.2
  359.6 87.0 all-gather.4
  450.7 87.3 all-reduce.1
where the time goes:
time: 548 us; the launch traced here: 546 us
  waiting for transfers between devices  309 us (56%)
  starting transfers between devices  98.8 us (18%)
  matrix products  34.2 us (6%)
  other arithmetic  30.6 us (6%)
  blocking collectives  29.8 us (5%)
  local copies, waits for them, and re-layouts  29.6 us (5%)
  between operations  14.4 us (3%)
    ppermute x22, waiting for transfers between devices, shifted(): return lax.ppermute(block, axis, route)  115 us
    ppermute x22, starting transfers between devices, shifted(): return lax.ppermute(block, axis, route)  98.7 us
    psum x1, waiting for transfers between devices, local(): grad_conv = lax.psum(kernel_terms, ('seq', 'rep'))  84.3 us
    all_gather x1, waiting for transfers between devices, local(): lax.all_gather(value_weight, ('seq', 'rep'), axis=0, tiled=True)  75.3 us
    all_gather x1, waiting for transfers between devices, local(): lax.all_gather(grad_value, ('seq', 'rep'), axis=0, tiled=True)  33.6 us
    all_to_all x1, blocking collectives, local(): feature_rows = lax.all_to_all(gathered, ('seq', 'rep'), 1, 0, tiled=True)  29.8 us
    add x10, other arithmetic, chain_join(): following[0][:, None, None] * earlier[1] + following[1]  12.7 us
  transfers between devices with their start and end apart: 25, of which 16 were waited for; matrix products, arithmetic and copies ran while one was open for 12% of the time, Pallas kernels for 0%

commit v1 on v0

--- a/solution.py
+++ b/solution.py
@@ -1,10 +1,39 @@
+import functools
 import math
 import jax
 import jax.numpy as jnp
 from jax import lax
 from jax.sharding import PartitionSpec as P
+from jax.lax import axis_index, ppermute, psum
 
 EPSILON = 1e-06
+
+
+def link_the_state(m, on_dim):
+    m = jnp.moveaxis(m, 0, on_dim)
+    b_next = m.shape
+    return m.reshape(*b_next[:on_dim], b_next[on_dim] * b_next[on_dim + 1], *b_next[on_dim + 2 :])
+
+
+def spans_number(w_in, chip_axis, k_dim):
+    n_shards = psum(1, chip_axis)
+    xs_all = [(src_i, (src_i + 1) % n_shards) for src_i in range(n_shards)]
+    o_now, local_next = ([], [])
+    tick = 0
+    sides = [(nth, j) for j, nth in xs_all]
+    while tick < n_shards - 1:
+        if tick % 2 == 0:
+            o_now.append(ppermute(o_now[-1] if o_now else w_in, chip_axis, xs_all))
+        else:
+            local_next.append(ppermute(local_next[-1] if local_next else w_in, chip_axis, sides))
+        tick += 1
+    block_out = jnp.stack([*o_now[::-1], w_in, *local_next], 0)
+    b_now = axis_index(chip_axis) - len(o_now)
+    block_out = block_out[(jnp.arange(n_shards) - b_now) % n_shards]
+    return link_the_state(block_out, k_dim)
+
+
+order_cells = functools.partial(spans_number, chip_axis=("seq", "rep"), k_dim=0)
 
 
 def shifted(block, axis, distance):
@@ -113,11 +142,7 @@
     key_rows = key_in[0]
     gathered = lax.all_gather(activations, "head", axis=2, tiled=True)[0]
     columns = gathered
-    value_f32 = jnp.dot(
-        columns,
-        lax.all_gather(value_weight, ("seq", "rep"), axis=0, tiled=True),
-        preferred_element_type=jnp.float32,
-    )
+    value_f32 = jnp.dot(columns, order_cells(value_weight), preferred_element_type=jnp.float32)
     value_raw = value_f32.astype(jnp.bfloat16)
     before_all = shifted(
         jnp.stack(

time: 548 us -> 682 us (1.24)
  starting transfers between devices: 98.8 us -> 161 us
  waiting for transfers between devices: 309 us -> 344 us
  local copies, waits for them, and re-layouts: 29.6 us -> 57.6 us
    ppermute x0 -> x15, waiting for transfers between devices: none -> 118 us  [the longest x8 65.4 us: spans_number(): o_now.append(ppermute(o_now[-1] if o_now else w_in, chip_axis, xs_all))]
    all_gather x1, waiting for transfers between devices: 75.3 us -> 0.02 us  [local(): lax.all_gather(value_weight, ('seq', 'rep'), axis=0, tiled=True)]
    ppermute x0 -> x15, starting transfers between devices: none -> 50.5 us  [the longest x8 46.5 us: spans_number(): o_now.append(ppermute(o_now[-1] if o_now else w_in, chip_axis, xs_all))]
    unnamed x56 -> x63, local copies, waits for them, and re-layouts: 7.99 us -> 26 us
    ppermute x22, starting transfers between devices: 98.7 us -> 110 us  [shifted(): return lax.ppermute(block, axis, route)]
    gather x0 -> x1, local copies, waits for them, and re-layouts: none -> 8.43 us  [spans_number(): block_out = block_out[(jnp.arange(n_shards) - b_now) % n_shards]]
  transfers between devices with their start and end apart: 25 -> 40, of which waited for: 16 -> 24; matrix products, arithmetic and copies ran while one was open for 12% -> 19% of each run, Pallas kernels for 0% -> 0%
where the time goes in v1:
time: 682 us; the launch traced here: 680 us
  waiting for transfers between devices  344 us (50%)
  starting transfers between devices  161 us (24%)
  local copies, waits for them, and re-layouts  57.6 us (8%)
  matrix products  38.3 us (6%)
  other arithmetic  33.6 us (5%)
  blocking collectives  30.9 us (5%)
  between operations  14.4 us (2%)
    ppermute x22, starting transfers between devices, shifted(): return lax.ppermute(block, axis, route)  110 us
    ppermute x22, waiting for transfers between devices, shifted(): return lax.ppermute(block, axis, route)  109 us
    psum x1, waiting for transfers between devices, local(): grad_conv = lax.psum(kernel_terms, ('seq', 'rep'))  84.3 us
    ppermute x8, waiting for transfers between devices, spans_number(): o_now.append(ppermute(o_now[-1] if o_now else w_in, chip_axis, xs_all))  65.4 us
    ppermute x7, waiting for transfers between devices, spans_number(): ppermute(local_next[-1] if local_next else w_in, chip_axis, sides)  52.7 us
    ppermute x8, starting transfers between devices, spans_number(): o_now.append(ppermute(o_now[-1] if o_now else w_in, chip_axis, xs_all))  46.5 us
    all_gather x1, waiting for transfers between devices, local(): lax.all_gather(grad_value, ('seq', 'rep'), axis=0, tiled=True)  32.6 us
    all_to_all x1, blocking collectives, local(): feature_rows = lax.all_to_all(gathered, ('seq', 'rep'), 1, 0, tiled=True)  30.9 us
  transfers between devices with their start and end apart: 40, of which 24 were waited for; matrix products, arithmetic and copies ran while one was open for 19% of the time, Pallas kernels for 0%

profile of v1, /device:TPU:0, one launch (start us, length us, event | category | flops | bytes accessed | tf_op | source)
XLA Modules:
  0.0 679.6 jit_solution(14391786329677099267)
XLA Ops:
  7.2 3.0 collective-permute-start.2
  10.2 11.5 %collective-permute-done.2 = bf16[128,2048]{1,0:T(8,128)(2,1)S(1)} collective-permute-done((bf16[128,2048]{1,0:T(8,128)(2,1)}, bf16[128,2048]{1,0:T(8,128)(2,1)S(1)}, u32[]{:S(2)}, u32[]{:S(2)}) %collective-permute-start.2) | collective-permute-done | bytes 524320 | tf_op jit(solution)/shard_map/ppermute | solution.py:26
  26.2 15.9 %collective-permute-done.3 = bf16[128,2048]{1,0:T(8,128)(2,1)S(1)} collective-permute-done((bf16[128,2048]{1,0:T(8,128)(2,1)S(1)}, bf16[128,2048]{1,0:T(8,128)(2,1)S(1)}, u32[]{:S(2)}, u32[]{:S(2)}) %collective-permute-start.3) | collective-permute-done | bytes 524320 | tf_op jit(solution)/shard_map/ppermute | solution.py:26
  44.5 10.1 %collective-permute-done.10 = bf16[128,2048]{1,0:T(8,128)(2,1)S(1)} collective-permute-done((bf16[128,2048]{1,0:T(8,128)(2,1)}, bf16[128,2048]{1,0:T(8,128)(2,1)S(1)}, u32[]{:S(2)}, u32[]{:S(2)}) %collective-permute-start.10) | collective-permute-done | bytes 524320 | tf_op jit(solution)/shard_map/ppermute | solution.py:28
  56.9 8.0 %collective-permute-start.5 = (bf16[128,2048]{1,0:T(8,128)(2,1)S(1)}, bf16[128,2048]{1,0:T(8,128)(2,1)S(1)}, u32[]{:S(2)}, u32[]{:S(2)}) collective-permute-start(bf16[128,2048]{1,0:T(8,128)(2,1)S(1)} %collective-permute-done.4), channel_id=1, source_target_pairs={{0,1},{1,2},{2,3},{3,4},{4,5},{5,6},{6,7},{7,8},{8,9},{9,10},{10,1... | collective-permute-start | bytes 1572872 | tf_op jit(solution)/shard_map/ppermute | solution.py:26
  64.8 13.5 %collective-permute-done.11 = bf16[128,2048]{1,0:T(8,128)(2,1)S(1)} collective-permute-done((bf16[128,2048]{1,0:T(8,128)(2,1)S(1)}, bf16[128,2048]{1,0:T(8,128)(2,1)S(1)}, u32[]{:S(2)}, u32[]{:S(2)}) %collective-permute-start.11) | collective-permute-done | bytes 524320 | tf_op jit(solution)/shard_map/ppermute | solution.py:28
  78.4 8.9 %collective-permute-start.6 = (bf16[128,2048]{1,0:T(8,128)(2,1)S(1)}, bf16[128,2048]{1,0:T(8,128)(2,1)S(1)}, u32[]{:S(2)}, u32[]{:S(2)}) collective-permute-start(bf16[128,2048]{1,0:T(8,128)(2,1)S(1)} %collective-permute-done.5), channel_id=1, source_target_pairs={{0,1},{1,2},{2,3},{3,4},{4,5},{5,6},{6,7},{7,8},{8,9},{9,10},{10,1... | collective-permute-start | bytes 1572872 | tf_op jit(solution)/shard_map/ppermute | solution.py:26
  87.3 13.5 %collective-permute-done.12 = bf16[128,2048]{1,0:T(8,128)(2,1)S(1)} collective-permute-done((bf16[128,2048]{1,0:T(8,128)(2,1)S(1)}, bf16[128,2048]{1,0:T(8,128)(2,1)S(1)}, u32[]{:S(2)}, u32[]{:S(2)}) %collective-permute-start.12) | collective-permute-done | bytes 524320 | tf_op jit(solution)/shard_map/ppermute | solution.py:28
  101.6 13.8 %collective-permute-start.7 = (bf16[128,2048]{1,0:T(8,128)(2,1)S(1)}, bf16[128,2048]{1,0:T(8,128)(2,1)}, u32[]{:S(2)}, u32[]{:S(2)}) collective-permute-start(bf16[128,2048]{1,0:T(8,128)(2,1)S(1)} %collective-permute-done.6), channel_id=1, source_target_pairs={{0,1},{1,2},{2,3},{3,4},{4,5},{5,6},{6,7},{7,8},{8,9},{9,10},{10,1... | collective-permute-start | bytes 1572872 | tf_op jit(solution)/shard_map/ppermute | solution.py:26
  115.4 9.1 %collective-permute-done.13 = bf16[128,2048]{1,0:T(8,128)(2,1)} collective-permute-done((bf16[128,2048]{1,0:T(8,128)(2,1)S(1)}, bf16[128,2048]{1,0:T(8,128)(2,1)}, u32[]{:S(2)}, u32[]{:S(2)}) %collective-permute-start.13) | collective-permute-done | bytes 524320 | tf_op jit(solution)/shard_map/ppermute | solution.py:28
  124.5 8.8 %collective-permute-done.7 = bf16[128,2048]{1,0:T(8,128)(2,1)} collective-permute-done((bf16[128,2048]{1,0:T(8,128)(2,1)S(1)}, bf16[128,2048]{1,0:T(8,128)(2,1)}, u32[]{:S(2)}, u32[]{:S(2)}) %collective-permute-start.7) | collective-permute-done | bytes 524320 | tf_op jit(solution)/shard_map/ppermute | solution.py:26
  133.3 2.6 collective-permute-start.8
  140.6 13.4 %collective-permute-done.8 = bf16[128,2048]{1,0:T(8,128)(2,1)} collective-permute-done((bf16[128,2048]{1,0:T(8,128)(2,1)}, bf16[128,2048]{1,0:T(8,128)(2,1)}, u32[]{:S(2)}, u32[]{:S(2)}) %collective-permute-start.8) | collective-permute-done | bytes 524320 | tf_op jit(solution)/shard_map/ppermute | solution.py:26
  154.1 5.4 collective-permute-start.9
  160.6 6.5 collective-permute-done.15
  167.1 13.6 %collective-permute-done.9 = bf16[128,2048]{1,0:T(8,128)(2,1)S(1)} collective-permute-done((bf16[128,2048]{1,0:T(8,128)(2,1)}, bf16[128,2048]{1,0:T(8,128)(2,1)S(1)}, u32[]{:S(2)}, u32[]{:S(2)}) %collective-permute-start.9) | collective-permute-done | bytes 524320 | tf_op jit(solution)/shard_map/ppermute | solution.py:26
  200.5 8.4 %gather_fusion = bf16[16,128,2048]{2,1,0:T(8,128)(2,1)} fusion(bf16[16,128,2048]{2,1,0:T(8,128)(2,1)} %bitcast_dynamic-update-slice_fusion, s32[1024]{0:T(1024)S(1)} %pad_clamp_fusion), kind=kCustom, calls=%fused_computation | custom fusion | bytes 16777280 | tf_op jit(solution)/shard_map/gather | solution.py:32
  208.9 4.7 fusion.2
  213.8 15.7 %collective-permute-start.17 = (bf16[3,3,2048]{2,1,0:T(4,128)(2,1)S(1)}, bf16[3,3,2048]{2,1,0:T(4,128)(2,1)S(1)}, u32[]{:S(2)}, u32[]{:S(2)}) collective-permute-start(bf16[3,3,2048]{2,1,0:T(4,128)(2,1)S(1)} %pad_maximum_fusion.5), channel_id=1, source_target_pairs={{0,2},{2,4},{4,6},{6,8},{8,10},{10,12},{12,14},{1,3},{3,5},{5,7},{... | collective-permute-start | bytes 110600 | tf_op jit(solution)/shard_map/ppermute | solution.py:42
  237.1 3.1 collective-permute-start.18
  244.3 16.6 %collective-permute-start.19 = (f32[16,128,128]{2,1,0:T(8,128)S(1)}, f32[16,128,128]{2,1,0:T(8,128)S(1)}, u32[]{:S(2)}, u32[]{:S(2)}) collective-permute-start(f32[16,128,128]{2,1,0:T(8,128)S(1)} %get-tuple-element.65), channel_id=1, source_target_pairs={{0,4},{2,6},{4,8},{6,10},{8,12},{10,14},{1,5},{3,7},{5,9},{7,11},{... | collective-permute-start | bytes 3145736 | tf_op jit(solution)/shard_map/ppermute | solution.py:42
  263.7 3.9 collective-permute-done.22
  267.6 14.4 %collective-permute-done.25 = f32[16,128,128]{2,1,0:T(8,128)S(1)} collective-permute-done((f32[16,128,128]{2,1,0:T(8,128)S(1)}, f32[16,128,128]{2,1,0:T(8,128)S(1)}, u32[]{:S(2)}, u32[]{:S(2)}) %collective-permute-start.25) | collective-permute-done | bytes 1048608 | tf_op jit(solution)/shard_map/ppermute | solution.py:42
  285.7 7.5 %collective-permute-start.20 = (f32[16,128,128]{2,1,0:T(8,128)}, f32[16,128,128]{2,1,0:T(8,128)}, u32[]{:S(2)}, u32[]{:S(2)}) collective-permute-start(f32[16,128,128]{2,1,0:T(8,128)} %multiply_add_fusion.10), channel_id=1, source_target_pairs={{0,8},{2,10},{4,12},{6,14},{1,9},{3,11},{5,13},{7,15},{16,24},{18,... | collective-permute-start | bytes 3145736 | tf_op jit(solution)/shard_map/ppermute | solution.py:42
  295.4 4.5 collective-permute-start.1
  301.2 13.9 %collective-permute-done.1 = f32[16]{0:T(128)S(1)} collective-permute-done((f32[16]{0:T(128)S(1)}, f32[16]{0:T(128)S(1)}, u32[]{:S(2)}, u32[]{:S(2)}) %collective-permute-start.1) | collective-permute-done | bytes 96 | tf_op jit(solution)/shard_map/ppermute | solution.py:42
  320.2 13.9 %collective-permute-done.26 = f32[16,128,128]{2,1,0:T(8,128)} collective-permute-done((f32[16,128,128]{2,1,0:T(8,128)}, f32[16,128,128]{2,1,0:T(8,128)}, u32[]{:S(2)}, u32[]{:S(2)}) %collective-permute-start.26) | collective-permute-done | bytes 1048608 | tf_op jit(solution)/shard_map/ppermute | solution.py:42
  338.9 3.2 collective-permute-start.21
  348.2 16.3 %collective-permute-start.28 = (f32[16,128,128]{2,1,0:T(8,128)S(1)}, f32[16,128,128]{2,1,0:T(8,128)S(1)}, u32[]{:S(2)}, u32[]{:S(2)}) collective-permute-start(f32[16,128,128]{2,1,0:T(8,128)S(1)} %fusion.54), channel_id=1, source_target_pairs={{0,2},{2,4},{4,6},{6,8},{8,10},{10,12},{12,14},{1,3},{3,5},{5,7},{... | collective-permute-start | bytes 3145736 | tf_op jit(solution)/shard_map/ppermute | solution.py:42
  368.6 16.9 %collective-permute-start.29 = (f32[16,128,128]{2,1,0:T(8,128)S(1)}, f32[16,128,128]{2,1,0:T(8,128)S(1)}, u32[]{:S(2)}, u32[]{:S(2)}) collective-permute-start(f32[16,128,128]{2,1,0:T(8,128)S(1)} %get-tuple-element.61), channel_id=1, source_target_pairs={{0,4},{2,6},{4,8},{6,10},{8,12},{10,14},{1,5},{3,7},{5,9},{7,11},{... | collective-permute-start | bytes 3145736 | tf_op jit(solution)/shard_map/ppermute | solution.py:42
  386.4 20.4 %collective-permute-done.33 = f32[16,128,128]{2,1,0:T(8,128)S(1)} collective-permute-done((f32[16,128,128]{2,1,0:T(8,128)S(1)}, f32[16,128,128]{2,1,0:T(8,128)S(1)}, u32[]{:S(2)}, u32[]{:S(2)}) %collective-permute-start.33) | collective-permute-done | bytes 1048608 | tf_op jit(solution)/shard_map/ppermute | solution.py:42
  410.5 7.5 %collective-permute-start.30 = (f32[16,128,128]{2,1,0:T(8,128)}, f32[16,128,128]{2,1,0:T(8,128)}, u32[]{:S(2)}, u32[]{:S(2)}) collective-permute-start(f32[16,128,128]{2,1,0:T(8,128)} %multiply_add_fusion.4), channel_id=1, source_target_pairs={{0,8},{2,10},{4,12},{6,14},{1,9},{3,11},{5,13},{7,15},{16,24},{18,... | collective-permute-start | bytes 3145736 | tf_op jit(solution)/shard_map/ppermute | solution.py:42
  423.6 34.6 %collective-permute-done.34 = f32[16,128,128]{2,1,0:T(8,128)} collective-permute-done((f32[16,128,128]{2,1,0:T(8,128)}, f32[16,128,128]{2,1,0:T(8,128)}, u32[]{:S(2)}, u32[]{:S(2)}) %collective-permute-start.34) | collective-permute-done | bytes 1048608 | tf_op jit(solution)/shard_map/ppermute | solution.py:42
  462.9 3.1 collective-permute-start.31
  466.0 2.5 convolution_bitcast_fusion
  474.3 3.1 fusion.92
  481.6 2.6 copy.159
  484.1 2.5 collective-permute-done.36
  486.7 4.5 multiply_reduce_fusion.3
  492.6 30.9 %all_to_all.19 = bf16[128,16,128]{0,2,1:T(8,128)(2,1)S(1)} all-to-all(bf16[128,16,128]{0,2,1:T(8,128)(2,1)S(1)} %bitcast.238), channel_id=1, replica_groups=mesh['parts'=2,'seq'=8,'rep'=2,'head'=1] {'seq','rep'}, dimensions={1} | all-to-all | bytes 1048576 | tf_op jit(solution)/shard_map/all_to_all | solution.py:288
  523.8 2.6 copy.113
  528.4 2.5 copy.126
  531.0 4.2 multiply_reduce_fusion.11
  535.2 4.4 multiply_reduce_fusion.7
  540.5 7.1 %fusion.1 = bf16[1,128,2048]{2,1,0:T(8,128)(2,1)} fusion(bf16[128,2048]{1,0:T(8,128)(2,1)S(1)} %copy-done.8, bf16[2048,2048]{1,0:T(8,128)(2,1)} %all-gather.3.cloned.1.call-done), kind=kOutput, calls=%fused_computation.5 | convolution fusion | flops 1074003968 | bytes 9437184 | tf_op jit(solution)/shard_map/dot_general | solution.py:279
  547.5 32.6 %all-gather.5.cloned.1.call-done = bf16[2048,2048]{1,0:T(8,128)(2,1)} async-done(((bf16[128,2048]{1,0:T(8,128)(2,1)}), bf16[2048,2048]{1,0:T(8,128)(2,1)}) %all-gather.5.cloned.1.call-update) | async-done | bytes 8388624 | tf_op jit(solution)/shard_map/all_gather | solution.py:289
  580.1 5.8 fusion
  587.2 84.3 %all-reduce.2.cloned.1.call-done = f32[3,4,2048]{2,1,0:T(4,128)} async-done(((f32[3,4,2048]{2,1,0:T(4,128)}), f32[3,4,2048]{2,1,0:T(4,128)}) %all-reduce.2.cloned.1.call-update) | async-done | bytes 98320 | tf_op jit(solution)/shard_map/psum | solution.py:278
  (176 shorter events, 109.3 us)
Async XLA Ops:
  7.2 184.5 %copy-start.12 = (bf16[128,2048]{1,0:T(8,128)(2,1)S(1)}, bf16[128,2048]{1,0:T(8,128)(2,1)}, u32[]{:S(2)}) copy-start(bf16[128,2048]{1,0:T(8,128)(2,1)} %param.8) | copy-start | bytes 1572868
  7.2 533.3 %all-gather.3.cloned.1.call-start = ((), (), s32[]{:S(2)}) async-start(), calls=%async_computation.1 | async-start | bytes 8912896 | tf_op jit(solution)/shard_map/all_gather | solution.py:281
  7.2 14.5 %collective-permute-start.2 = (bf16[128,2048]{1,0:T(8,128)(2,1)}, bf16[128,2048]{1,0:T(8,128)(2,1)S(1)}, u32[]{:S(2)}, u32[]{:S(2)}) collective-permute-start(bf16[128,2048]{1,0:T(8,128)(2,1)} %param.8), channel_id=1, source_target_pairs={{0,1},{1,2},{2,3},{3,4},{4,5},{5,6},{6,7},{7,8},{8,9},{9,10},{10,1... | collective-permute-start | bytes 1572872 | tf_op jit(solution)/shard_map/ppermute | solution.py:26
  21.7 20.3 %collective-permute-start.3 = (bf16[128,2048]{1,0:T(8,128)(2,1)S(1)}, bf16[128,2048]{1,0:T(8,128)(2,1)S(1)}, u32[]{:S(2)}, u32[]{:S(2)}) collective-permute-start(bf16[128,2048]{1,0:T(8,128)(2,1)S(1)} %collective-permute-done.2), channel_id=1, source_target_pairs={{0,1},{1,2},{2,3},{3,4},{4,5},{5,6},{6,7},{7,8},{8,9},{9,10},{10,1... | collective-permute-start | bytes 1572872 | tf_op jit(solution)/shard_map/ppermute | solution.py:26
  24.1 30.5 %collective-permute-start.10 = (bf16[128,2048]{1,0:T(8,128)(2,1)}, bf16[128,2048]{1,0:T(8,128)(2,1)S(1)}, u32[]{:S(2)}, u32[]{:S(2)}) collective-permute-start(bf16[128,2048]{1,0:T(8,128)(2,1)} %param.8), channel_id=1, source_target_pairs={{1,0},{2,1},{3,2},{4,3},{5,4},{6,5},{7,6},{8,7},{9,8},{10,9},{11,1... | collective-permute-start | bytes 1572872 | tf_op jit(solution)/shard_map/ppermute | solution.py:28
  42.1 14.8 %collective-permute-start.4 = (bf16[128,2048]{1,0:T(8,128)(2,1)S(1)}, bf16[128,2048]{1,0:T(8,128)(2,1)S(1)}, u32[]{:S(2)}, u32[]{:S(2)}) collective-permute-start(bf16[128,2048]{1,0:T(8,128)(2,1)S(1)} %collective-permute-done.3), channel_id=1, source_target_pairs={{0,1},{1,2},{2,3},{3,4},{4,5},{5,6},{6,7},{7,8},{8,9},{9,10},{10,1... | collective-permute-start | bytes 1572872 | tf_op jit(solution)/shard_map/ppermute | solution.py:26
  54.6 23.7 %collective-permute-start.11 = (bf16[128,2048]{1,0:T(8,128)(2,1)S(1)}, bf16[128,2048]{1,0:T(8,128)(2,1)S(1)}, u32[]{:S(2)}, u32[]{:S(2)}) collective-permute-start(bf16[128,2048]{1,0:T(8,128)(2,1)S(1)} %collective-permute-done.10), channel_id=1, source_target_pairs={{1,0},{2,1},{3,2},{4,3},{5,4},{6,5},{7,6},{8,7},{9,8},{10,9},{11,1... | collective-permute-start | bytes 1572872 | tf_op jit(solution)/shard_map/ppermute | solution.py:28
  56.9 21.5 %collective-permute-start.5 = (bf16[128,2048]{1,0:T(8,128)(2,1)S(1)}, bf16[128,2048]{1,0:T(8,128)(2,1)S(1)}, u32[]{:S(2)}, u32[]{:S(2)}) collective-permute-start(bf16[128,2048]{1,0:T(8,128)(2,1)S(1)} %collective-permute-done.4), channel_id=1, source_target_pairs={{0,1},{1,2},{2,3},{3,4},{4,5},{5,6},{6,7},{7,8},{8,9},{9,10},{10,1... | collective-permute-start | bytes 1572872 | tf_op jit(solution)/shard_map/ppermute | solution.py:26
  78.4 22.5 %collective-permute-start.12 = (bf16[128,2048]{1,0:T(8,128)(2,1)S(1)}, bf16[128,2048]{1,0:T(8,128)(2,1)S(1)}, u32[]{:S(2)}, u32[]{:S(2)}) collective-permute-start(bf16[128,2048]{1,0:T(8,128)(2,1)S(1)} %collective-permute-done.11), channel_id=1, source_target_pairs={{1,0},{2,1},{3,2},{4,3},{5,4},{6,5},{7,6},{8,7},{9,8},{10,9},{11,1... | collective-permute-start | bytes 1572872 | tf_op jit(solution)/shard_map/ppermute | solution.py:28
  78.4 46.1 %copy-start.20 = (bf16[128,2048]{1,0:T(8,128)(2,1)}, bf16[128,2048]{1,0:T(8,128)(2,1)S(1)}, u32[]{:S(2)}) copy-start(bf16[128,2048]{1,0:T(8,128)(2,1)S(1)} %collective-permute-done.5) | copy-start | bytes 1572868
  78.4 23.3 %collective-permute-start.6 = (bf16[128,2048]{1,0:T(8,128)(2,1)S(1)}, bf16[128,2048]{1,0:T(8,128)(2,1)S(1)}, u32[]{:S(2)}, u32[]{:S(2)}) collective-permute-start(bf16[128,2048]{1,0:T(8,128)(2,1)S(1)} %collective-permute-done.5), channel_id=1, source_target_pairs={{0,1},{1,2},{2,3},{3,4},{4,5},{5,6},{6,7},{7,8},{8,9},{9,10},{10,1... | collective-permute-start | bytes 1572872 | tf_op jit(solution)/shard_map/ppermute | solution.py:26
  101.6 22.9 %collective-permute-start.13 = (bf16[128,2048]{1,0:T(8,128)(2,1)S(1)}, bf16[128,2048]{1,0:T(8,128)(2,1)}, u32[]{:S(2)}, u32[]{:S(2)}) collective-permute-start(bf16[128,2048]{1,0:T(8,128)(2,1)S(1)} %collective-permute-done.12), channel_id=1, source_target_pairs={{1,0},{2,1},{3,2},{4,3},{5,4},{6,5},{7,6},{8,7},{9,8},{10,9},{11,1... | collective-permute-start | bytes 1572872 | tf_op jit(solution)/shard_map/ppermute | solution.py:28
  101.6 31.7 %collective-permute-start.7 = (bf16[128,2048]{1,0:T(8,128)(2,1)S(1)}, bf16[128,2048]{1,0:T(8,128)(2,1)}, u32[]{:S(2)}, u32[]{:S(2)}) collective-permute-start(bf16[128,2048]{1,0:T(8,128)(2,1)S(1)} %collective-permute-done.6), channel_id=1, source_target_pairs={{0,1},{1,2},{2,3},{3,4},{4,5},{5,6},{6,7},{7,8},{8,9},{9,10},{10,1... | collective-permute-start | bytes 1572872 | tf_op jit(solution)/shard_map/ppermute | solution.py:26
  124.5 14.3 %collective-permute-start.14 = (bf16[128,2048]{1,0:T(8,128)(2,1)}, bf16[128,2048]{1,0:T(8,128)(2,1)}, u32[]{:S(2)}, u32[]{:S(2)}) collective-permute-start(bf16[128,2048]{1,0:T(8,128)(2,1)} %collective-permute-done.13), channel_id=1, source_target_pairs={{1,0},{2,1},{3,2},{4,3},{5,4},{6,5},{7,6},{8,7},{9,8},{10,9},{11,1... | collective-permute-start | bytes 1572872 | tf_op jit(solution)/shard_map/ppermute | solution.py:28
  133.3 20.7 %collective-permute-start.8 = (bf16[128,2048]{1,0:T(8,128)(2,1)}, bf16[128,2048]{1,0:T(8,128)(2,1)}, u32[]{:S(2)}, u32[]{:S(2)}) collective-permute-start(bf16[128,2048]{1,0:T(8,128)(2,1)} %collective-permute-done.7), channel_id=1, source_target_pairs={{0,1},{1,2},{2,3},{3,4},{4,5},{5,6},{6,7},{7,8},{8,9},{9,10},{10,1... | collective-permute-start | bytes 1572872 | tf_op jit(solution)/shard_map/ppermute | solution.py:26
  135.9 444.2 %all-gather.5.cloned.1.call-start = ((), (), s32[]{:S(2)}) async-start(), calls=%async_computation.2 | async-start | bytes 8912896 | tf_op jit(solution)/shard_map/all_gather | solution.py:289
  138.5 55.7 %copy-start.19 = (bf16[128,2048]{1,0:T(8,128)(2,1)S(1)}, bf16[128,2048]{1,0:T(8,128)(2,1)}, u32[]{:S(2)}) copy-start(bf16[128,2048]{1,0:T(8,128)(2,1)} %copy-done.18) | copy-start | bytes 1572868
  138.7 28.4 %collective-permute-start.15 = (bf16[128,2048]{1,0:T(8,128)(2,1)}, bf16[128,2048]{1,0:T(8,128)(2,1)S(1)}, u32[]{:S(2)}, u32[]{:S(2)}) collective-permute-start(bf16[128,2048]{1,0:T(8,128)(2,1)} %collective-permute-done.14), channel_id=1, source_target_pairs={{1,0},{2,1},{3,2},{4,3},{5,4},{6,5},{7,6},{8,7},{9,8},{10,9},{11,1... | collective-permute-start | bytes 1572872 | tf_op jit(solution)/shard_map/ppermute | solution.py:28
  154.1 26.7 %collective-permute-start.9 = (bf16[128,2048]{1,0:T(8,128)(2,1)}, bf16[128,2048]{1,0:T(8,128)(2,1)S(1)}, u32[]{:S(2)}, u32[]{:S(2)}) collective-permute-start(bf16[128,2048]{1,0:T(8,128)(2,1)} %collective-permute-done.8), channel_id=1, source_target_pairs={{0,1},{1,2},{2,3},{3,4},{4,5},{5,6},{6,7},{7,8},{8,9},{9,10},{10,1... | collective-permute-start | bytes 1572872 | tf_op jit(solution)/shard_map/ppermute | solution.py:26
  167.1 32.5 %collective-permute-start.16 = (bf16[128,2048]{1,0:T(8,128)(2,1)S(1)}, bf16[128,2048]{1,0:T(8,128)(2,1)S(1)}, u32[]{:S(2)}, u32[]{:S(2)}) collective-permute-start(bf16[128,2048]{1,0:T(8,128)(2,1)S(1)} %collective-permute-done.15), channel_id=1, source_target_pairs={{1,0},{2,1},{3,2},{4,3},{5,4},{6,5},{7,6},{8,7},{9,8},{10,9},{11,1... | collective-permute-start | bytes 1572872 | tf_op jit(solution)/shard_map/ppermute | solution.py:28
  213.8 16.6 %collective-permute-start.17 = (bf16[3,3,2048]{2,1,0:T(4,128)(2,1)S(1)}, bf16[3,3,2048]{2,1,0:T(4,128)(2,1)S(1)}, u32[]{:S(2)}, u32[]{:S(2)}) collective-permute-start(bf16[3,3,2048]{2,1,0:T(4,128)(2,1)S(1)} %pad_maximum_fusion.5), channel_id=1, source_target_pairs={{0,2},{2,4},{4,6},{6,8},{8,10},{10,12},{12,14},{1,3},{3,5},{5,7},{... | collective-permute-start | bytes 110600 | tf_op jit(solution)/shard_map/ppermute | solution.py:42
  233.9 51.8 %copy-start = (bf16[16,16,8,128]{3,2,1,0:T(8,128)(2,1)}, bf16[16,16,8,128]{3,2,1,0:T(8,128)(2,1)S(1)}, u32[]{:S(2)}) copy-start(bf16[16,16,8,128]{3,2,1,0:T(8,128)(2,1)S(1)} %fusion.71) | copy-start | bytes 1572868
  235.5 4.7 collective-permute-start.24
  237.1 5.3 collective-permute-start.18
  243.0 39.1 %collective-permute-start.25 = (f32[16,128,128]{2,1,0:T(8,128)S(1)}, f32[16,128,128]{2,1,0:T(8,128)S(1)}, u32[]{:S(2)}, u32[]{:S(2)}) collective-permute-start(f32[16,128,128]{2,1,0:T(8,128)S(1)} %get-tuple-element.66), channel_id=1, source_target_pairs={{4,0},{6,2},{8,4},{10,6},{12,8},{14,10},{5,1},{7,3},{9,5},{11,7},{... | collective-permute-start | bytes 3145736 | tf_op jit(solution)/shard_map/ppermute | solution.py:42
  244.3 40.3 %collective-permute-start.19 = (f32[16,128,128]{2,1,0:T(8,128)S(1)}, f32[16,128,128]{2,1,0:T(8,128)S(1)}, u32[]{:S(2)}, u32[]{:S(2)}) collective-permute-start(f32[16,128,128]{2,1,0:T(8,128)S(1)} %get-tuple-element.65), channel_id=1, source_target_pairs={{0,4},{2,6},{4,8},{6,10},{8,12},{10,14},{1,5},{3,7},{5,9},{7,11},{... | collective-permute-start | bytes 3145736 | tf_op jit(solution)/shard_map/ppermute | solution.py:42
  260.8 2.8 collective-permute-start
  262.4 5.3 collective-permute-start.22
  283.2 50.9 %collective-permute-start.26 = (f32[16,128,128]{2,1,0:T(8,128)}, f32[16,128,128]{2,1,0:T(8,128)}, u32[]{:S(2)}, u32[]{:S(2)}) collective-permute-start(f32[16,128,128]{2,1,0:T(8,128)} %multiply_add_fusion.7), channel_id=1, source_target_pairs={{8,0},{10,2},{12,4},{14,6},{9,1},{11,3},{13,5},{15,7},{24,16},{26,... | collective-permute-start | bytes 3145736 | tf_op jit(solution)/shard_map/ppermute | solution.py:42
  285.7 51.5 %collective-permute-start.20 = (f32[16,128,128]{2,1,0:T(8,128)}, f32[16,128,128]{2,1,0:T(8,128)}, u32[]{:S(2)}, u32[]{:S(2)}) collective-permute-start(f32[16,128,128]{2,1,0:T(8,128)} %multiply_add_fusion.10), channel_id=1, source_target_pairs={{0,8},{2,10},{4,12},{6,14},{1,9},{3,11},{5,13},{7,15},{16,24},{18,... | collective-permute-start | bytes 3145736 | tf_op jit(solution)/shard_map/ppermute | solution.py:42
  295.4 19.7 %collective-permute-start.1 = (f32[16]{0:T(128)S(1)}, f32[16]{0:T(128)S(1)}, u32[]{:S(2)}, u32[]{:S(2)}) collective-permute-start(f32[16]{0:T(128)S(1)} %get-tuple-element.63), channel_id=1, source_target_pairs={{0,4},{2,6},{4,8},{6,10},{8,12},{10,14},{1,5},{3,7},{5,9},{7,11},{... | collective-permute-start | bytes 200 | tf_op jit(solution)/shard_map/ppermute | solution.py:42
  299.9 15.2 %collective-permute-start.23 = (f32[16]{0:T(128)S(1)}, f32[16]{0:T(128)S(1)}, u32[]{:S(2)}, u32[]{:S(2)}) collective-permute-start(f32[16]{0:T(128)S(1)} %get-tuple-element.64), channel_id=1, source_target_pairs={{4,0},{6,2},{8,4},{10,6},{12,8},{14,10},{5,1},{7,3},{9,5},{11,7},{... | collective-permute-start | bytes 200 | tf_op jit(solution)/shard_map/ppermute | solution.py:42
  335.9 7.9 %collective-permute-start.27 = (bf16[16,128,128]{2,1,0:T(8,128)(2,1)S(1)}, bf16[16,128,128]{2,1,0:T(8,128)(2,1)S(1)}, u32[]{:S(2)}, u32[]{:S(2)}) collective-permute-start(bf16[16,128,128]{2,1,0:T(8,128)(2,1)S(1)} %multiply_add_fusion.6), channel_id=1, source_target_pairs={{2,0},{4,2},{6,4},{8,6},{10,8},{12,10},{14,12},{3,1},{5,3},{7,5},{... | collective-permute-start | bytes 1572872 | tf_op jit(solution)/shard_map/ppermute | solution.py:42
  338.9 5.2 collective-permute-start.21
  344.5 41.0 %copy-start.1 = (bf16[16,16,8,128]{3,2,1,0:T(8,128)(2,1)S(1)}, bf16[16,16,8,128]{3,2,1,0:T(8,128)(2,1)}, u32[]{:S(2)}) copy-start(bf16[16,16,8,128]{3,2,1,0:T(8,128)(2,1)} %copy-done) | copy-start | bytes 1572868
  345.8 72.6 %copy-start.5 = (bf16[128,16,128]{0,2,1:T(8,128)(2,1)}, bf16[128,16,128]{0,2,1:T(8,128)(2,1)S(1)}, u32[]{:S(2)}) copy-start(bf16[128,16,128]{0,2,1:T(8,128)(2,1)S(1)} %get-tuple-element.36) | copy-start | bytes 1572868
  346.8 71.2 %copy-start.4 = (bf16[128,2048]{0,1:T(8,128)(2,1)S(1)}, bf16[128,2048]{0,1:T(8,128)(2,1)}, u32[]{:S(2)}) copy-start(bf16[128,2048]{0,1:T(8,128)(2,1)} %copy.97) | copy-start | bytes 1572868
  346.8 17.9 %collective-permute-start.32 = (f32[16,128,128]{2,1,0:T(8,128)S(1)}, f32[16,128,128]{2,1,0:T(8,128)S(1)}, u32[]{:S(2)}, u32[]{:S(2)}) collective-permute-start(f32[16,128,128]{2,1,0:T(8,128)S(1)} %fusion.52), channel_id=1, source_target_pairs={{2,0},{4,2},{6,4},{8,6},{10,8},{12,10},{14,12},{3,1},{5,3},{7,5},{... | collective-permute-start | bytes 3145736 | tf_op jit(solution)/shard_map/ppermute | solution.py:42
  348.2 18.6 %collective-permute-start.28 = (f32[16,128,128]{2,1,0:T(8,128)S(1)}, f32[16,128,128]{2,1,0:T(8,128)S(1)}, u32[]{:S(2)}, u32[]{:S(2)}) collective-permute-start(f32[16,128,128]{2,1,0:T(8,128)S(1)} %fusion.54), channel_id=1, source_target_pairs={{0,2},{2,4},{4,6},{6,8},{8,10},{10,12},{12,14},{1,3},{3,5},{5,7},{... | collective-permute-start | bytes 3145736 | tf_op jit(solution)/shard_map/ppermute | solution.py:42
  367.3 39.5 %collective-permute-start.33 = (f32[16,128,128]{2,1,0:T(8,128)S(1)}, f32[16,128,128]{2,1,0:T(8,128)S(1)}, u32[]{:S(2)}, u32[]{:S(2)}) collective-permute-start(f32[16,128,128]{2,1,0:T(8,128)S(1)} %get-tuple-element.62), channel_id=1, source_target_pairs={{4,0},{6,2},{8,4},{10,6},{12,8},{14,10},{5,1},{7,3},{9,5},{11,7},{... | collective-permute-start | bytes 3145736 | tf_op jit(solution)/shard_map/ppermute | solution.py:42
  368.6 40.7 %collective-permute-start.29 = (f32[16,128,128]{2,1,0:T(8,128)S(1)}, f32[16,128,128]{2,1,0:T(8,128)S(1)}, u32[]{:S(2)}, u32[]{:S(2)}) collective-permute-start(f32[16,128,128]{2,1,0:T(8,128)S(1)} %get-tuple-element.61), channel_id=1, source_target_pairs={{0,4},{2,6},{4,8},{6,10},{8,12},{10,14},{1,5},{3,7},{5,9},{7,11},{... | collective-permute-start | bytes 3145736 | tf_op jit(solution)/shard_map/ppermute | solution.py:42
  408.1 50.1 %collective-permute-start.34 = (f32[16,128,128]{2,1,0:T(8,128)}, f32[16,128,128]{2,1,0:T(8,128)}, u32[]{:S(2)}, u32[]{:S(2)}) collective-permute-start(f32[16,128,128]{2,1,0:T(8,128)} %multiply_add_fusion.1), channel_id=1, source_target_pairs={{8,0},{10,2},{12,4},{14,6},{9,1},{11,3},{13,5},{15,7},{24,16},{26,... | collective-permute-start | bytes 3145736 | tf_op jit(solution)/shard_map/ppermute | solution.py:42
  410.5 50.7 %collective-permute-start.30 = (f32[16,128,128]{2,1,0:T(8,128)}, f32[16,128,128]{2,1,0:T(8,128)}, u32[]{:S(2)}, u32[]{:S(2)}) collective-permute-start(f32[16,128,128]{2,1,0:T(8,128)} %multiply_add_fusion.4), channel_id=1, source_target_pairs={{0,8},{2,10},{4,12},{6,14},{1,9},{3,11},{5,13},{7,15},{16,24},{18,... | collective-permute-start | bytes 3145736 | tf_op jit(solution)/shard_map/ppermute | solution.py:42
  422.0 46.5 %copy-start.2 = (bf16[16,16,8,128]{3,2,1,0:T(8,128)(2,1)S(1)}, bf16[16,16,8,128]{3,2,1,0:T(8,128)(2,1)}, u32[]{:S(2)}) copy-start(bf16[16,16,8,128]{3,2,1,0:T(8,128)(2,1)} %copy-done) | copy-start | bytes 1572868
  459.9 8.6 %collective-permute-start.35 = (bf16[16,128,128]{2,1,0:T(8,128)(2,1)S(1)}, bf16[16,128,128]{2,1,0:T(8,128)(2,1)S(1)}, u32[]{:S(2)}, u32[]{:S(2)}) collective-permute-start(bf16[16,128,128]{2,1,0:T(8,128)(2,1)S(1)} %multiply_add_fusion), channel_id=1, source_target_pairs={{2,0},{4,2},{6,4},{8,6},{10,8},{12,10},{14,12},{3,1},{5,3},{7,5},{... | collective-permute-start | bytes 1572872 | tf_op jit(solution)/shard_map/ppermute | solution.py:42
  462.9 6.1 collective-permute-start.31
  480.3 6.4 collective-permute-start.36
  491.2 180.3 %all-reduce.2.cloned.1.call-start = ((), (), s32[]{:S(2)}) async-start(), calls=%async_computation.3 | async-start | bytes 196608 | tf_op jit(solution)/shard_map/psum | solution.py:278
  (14 other events, 226.2 us)
Sparse Core Ops, SparseCore 0:
  136.1 92.0 all-gather.2
  491.4 88.7 all-gather.4
  584.1 87.2 all-reduce.1
